TPU v7x, 32 devices: a whole 2x2x4 slice. The times are simulated.
32 devices in a mesh: aux: 8 (over y, x, core), shell: 4 (over z).
Axes of the slice: x: 2, y: 2, z: 4, core: 2. Of those that a mesh axis runs over, the one named last changes fastest.
Arguments:
- density: bfloat16 [32, 120, 8192], P('aux', None, 'shell'), may hold values from -6 to 6
- occ_density: bfloat16 [32, 120, 120], P('aux'), may hold values from -6 to 6
- cabs_coeff: bfloat16 [2048, 8192], P('aux', 'shell'), may hold values from -0.0625 to 0.0625
- occ_coeff: bfloat16 [2048, 120], P('aux'), may hold values from -0.5 to 0.5
- tile_owner: int32 [16, 1], replicated, may hold values from 0 to 3; in each aligned block of 16 rows (0 to 15, 16 to 31, ...) at most 8 rows name the same one
Outputs:
- ao_density: bfloat16 [32, 32, 128, 2048], P('shell', 'aux')
Inputs may be any that keep to these rules, and one draw needn't show every extreme that they name: `tile_owner`: no owner holds more than 8 blocks, and some owner holds exactly 8; every owner holds at least one block.
All inputs are finite; a program needn't handle non-finite values.
Results may differ from a plain program's by a relative error of at most 0.015.
Values may be sent and summed in bfloat16 or wider, within the bound.
No kernel may reach another device: no remote copies, remote signals or barrier semaphores. Data moves between devices by JAX's collectives and lax.ppermute only.
A program may use at most 64 MiB of HBM per device.

v0:
```python
import jax
import jax.numpy as jnp
from jax import lax
from jax.sharding import PartitionSpec as P

NOCC = 120
CAPT = 8


def per_device(density, occ_density, cabs_coeff, occ_coeff, tile_owner):
    local_q = density.shape[0]
    owners = lax.axis_size("shell")
    me_shell = lax.axis_index("shell")
    occ_full = lax.all_gather(occ_coeff, "aux", axis=0, tiled=True)
    nao = occ_full.shape[0]
    ntile = tile_owner.shape[0]
    width = nao // ntile
    share_cols = nao // owners
    owned = (tile_owner[:, 0] == me_shell).astype(jnp.int32)
    rank = jnp.cumsum(owned) - 1
    select = (
        (rank[None, :] == jnp.arange(CAPT, dtype=jnp.int32)[:, None]) & (owned[None, :] == 1)
    ).astype(jnp.bfloat16)
    batches = 2
    span = local_q // batches
    results = []
    for batch in range(batches):
        dens = density[batch * span : (batch + 1) * span]
        occ_dens = occ_density[batch * span : (batch + 1) * span]
        flat = dens.reshape(span * NOCC, dens.shape[2])
        terms = lax.dot_general(
            flat,
            lax.all_gather(cabs_coeff, "aux", axis=0, tiled=True),
            (((1,), (1,)), ((), ())),
            preferred_element_type=jnp.float32,
        )
        mine = lax.psum_scatter(
            terms.astype(jnp.bfloat16), "shell", scatter_dimension=1, tiled=True
        ).astype(jnp.float32)
        my_rows = lax.dynamic_slice_in_dim(occ_full, me_shell * share_cols, share_cols, 0)
        occ_term = jnp.einsum("qij,nj->qin", occ_dens, my_rows, preferred_element_type=jnp.float32)
        rounded = (mine + occ_term.reshape(span * NOCC, share_cols)).astype(jnp.bfloat16)
        spread = lax.all_gather(rounded, "shell", axis=1, tiled=True)
        blocks = spread.reshape(span, NOCC, ntile, width)
        half_owned = jnp.einsum(
            "kt,qitw->kqiw", select, blocks, preferred_element_type=jnp.float32
        ).astype(jnp.bfloat16)
        gamma = jnp.einsum(
            "kqiw,mi->kqwm", half_owned, occ_full, preferred_element_type=jnp.float32
        )
        results.append(gamma.astype(jnp.bfloat16))
    return jnp.concatenate(results, axis=1)


def solution(mesh):
    in_specs = (
        P("aux", None, "shell"),
        P("aux", None, None),
        P("aux", "shell"),
        P("aux", None),
        P(),
    )
    out_specs = P("shell", "aux", None, None)
    return jax.shard_map(
        per_device, mesh=mesh, in_specs=in_specs, out_specs=out_specs, check_vma=False
    )
```

profile of v0, /device:TPU:0, one launch (start us, length us, event | category | flops | bytes accessed | tf_op | source)
XLA Modules:
  0.0 177.0 jit_solution(4344469540848584070)
XLA Ops:
  6.5 0.0 all-gather.2.cloned.1.call-start
  6.5 0.7 all-gather.2.cloned.1.call-update
  7.3 0.0 reduce-scatter.3.cloned.1.call-start
  7.3 1.6 fusion.26
  8.9 57.3 %all-gather.2.cloned.1.call-done = bf16[2048,2048]{1,0:T(8,128)(2,1)} async-done(((bf16[256,2048]{1,0:T(8,128)(2,1)}), bf16[2048,2048]{1,0:T(8,128)(2,1)}) %all-gather.2.cloned.1.call-update) | async-done | bytes 8388624 | tf_op jit(solution)/shard_map/all_gather | solution.py:33
  66.2 6.8 %convolution_convert_fusion.3 = bf16[240,2048]{1,0:T(8,128)(2,1)} fusion(bf16[240,2048]{1,0:T(8,128)(2,1)S(1)} %bitcast.57, bf16[2048,2048]{1,0:T(8,128)(2,1)} %all-gather.2.cloned.1.call-done), kind=kOutput, calls=%fused_computation.4 | convolution fusion | flops 2013757440 | bytes 10354688 | tf_op jit(solution)/shard_map/dot_general | solution.py:31
  73.0 0.0 copy-start.2
  73.0 0.0 reduce-scatter.3.cloned.1.call-update
  73.0 0.0 reduce-scatter.5.cloned.1.call-start
  73.1 6.7 %convolution_convert_fusion.2 = bf16[240,2048]{1,0:T(8,128)(2,1)} fusion(bf16[240,2048]{1,0:T(8,128)(2,1)S(1)} %bitcast.56, bf16[2048,2048]{1,0:T(8,128)(2,1)} %all-gather.2.cloned.1.call-done), kind=kOutput, calls=%fused_computation.3 | convolution fusion | flops 2013757440 | bytes 10354688 | tf_op jit(solution)/shard_map/dot_general | solution.py:31
  79.8 0.0 reduce-scatter.5.cloned.1.call-update
  79.8 0.0 copy-done.2
  79.9 0.1 copy.7
  80.0 0.0 copy-done.1
  80.0 10.9 %all_gather.14 = bf16[2048,120]{0,1:T(8,128)(2,1)S(1)} all-gather(bf16[256,120]{0,1:T(8,128)(2,1)S(1)} %copy-done.1), channel_id=1, replica_groups=mesh['aux'=8,'shell'=4] {'aux'}, dimensions={0}, use_global_device_ids=true | all-gather | bytes 552960 | tf_op jit(solution)/shard_map/all_gather | solution.py:14
  90.8 0.1 add_reduce_fusion
  91.0 0.0 copy-done
  91.0 0.2 fusion.8
  91.2 0.2 fusion.10
  91.4 8.0 %reduce-scatter.3.cloned.1.call-done = bf16[240,512]{1,0:T(8,128)(2,1)} async-done(((bf16[240,2048]{1,0:T(8,128)(2,1)}), bf16[240,512]{1,0:T(8,128)(2,1)}) %reduce-scatter.3.cloned.1.call-update) | async-done | bytes 245776 | tf_op jit(solution)/shard_map/reduce_scatter | solution.py:37
  99.5 1.0 fusion.5
  100.5 31.1 %all_gather.15 = bf16[240,2048]{1,0:T(8,128)(2,1)S(1)} all-gather(bf16[240,512]{1,0:T(8,128)(2,1)S(1)} %fusion.5), channel_id=1, replica_groups=mesh['aux'=8,'shell'=4] {'shell'}, dimensions={1}, use_global_device_ids=true | all-gather | bytes 1228800 | tf_op jit(solution)/shard_map/all_gather | solution.py:43
  131.5 0.2 copy.12
  131.8 4.9 %reduce-scatter.5.cloned.1.call-done = bf16[240,512]{1,0:T(8,128)(2,1)} async-done(((bf16[240,2048]{1,0:T(8,128)(2,1)}), bf16[240,512]{1,0:T(8,128)(2,1)}) %reduce-scatter.5.cloned.1.call-update) | async-done | bytes 245776 | tf_op jit(solution)/shard_map/reduce_scatter | solution.py:37
  136.7 1.0 fusion.4
  137.7 20.5 %all_gather.16 = bf16[240,2048]{1,0:T(8,128)(2,1)S(1)} all-gather(bf16[240,512]{1,0:T(8,128)(2,1)S(1)} %fusion.4), channel_id=1, replica_groups=mesh['aux'=8,'shell'=4] {'shell'}, dimensions={1}, use_global_device_ids=true | all-gather | bytes 1228800 | tf_op jit(solution)/shard_map/all_gather | solution.py:43
  158.2 0.2 copy.13
  158.4 0.3 fusion.2
  158.7 0.3 fusion
  159.0 2.4 %convolution_convert_fusion = bf16[8,2,128,2048]{3,2,1,0:T(8,128)(2,1)S(1)} fusion(bf16[8,2,120,128]{3,0,2,1:T(8,128)(2,1)S(1)} %fusion, bf16[2048,120]{0,1:T(8,128)(2,1)S(1)} %all_gather.14), kind=kOutput, calls=%fused_computation.1 | convolution fusion | flops 1010827264 | bytes 9371648 | tf_op jit(solution)/shard_map/kqiw,mi->kqwm/dot_general | solution.py:48
  161.4 2.4 %convolution_convert_fusion.1 = bf16[8,2,128,2048]{3,2,1,0:T(8,128)(2,1)S(1)} fusion(bf16[8,2,120,128]{3,0,2,1:T(8,128)(2,1)S(1)} %fusion.2, bf16[2048,120]{0,1:T(8,128)(2,1)S(1)} %all_gather.14), kind=kOutput, calls=%fused_computation.2 | convolution fusion | flops 1010827264 | bytes 9371648 | tf_op jit(solution)/shard_map/kqiw,mi->kqwm/dot_general | solution.py:48
  163.8 6.7 %pad_maximum_fusion = bf16[8,4,128,2048]{3,2,1,0:T(8,128)(2,1)} fusion(bf16[8,2,128,2048]{3,2,1,0:T(8,128)(2,1)S(1)} %convolution_convert_fusion, bf16[8,2,128,2048]{3,2,1,0:T(8,128)(2,1)S(1)} %convolution_convert_fusion.1), kind=kLoop, calls=%fused_computation | loop fusion | flops 8388608 | bytes 33554432 | tf_op jit(solution)/shard_map/concatenate | solution.py:52
  (4 shorter events, 0.0 us)
Async XLA Ops:
  6.5 59.7 %all-gather.2.cloned.1.call-start = ((), (), s32[]{:S(2)}) async-start(), calls=%async_computation.2 | async-start | bytes 9437184 | tf_op jit(solution)/shard_map/all_gather | solution.py:33
  7.3 92.2 %reduce-scatter.3.cloned.1.call-start = ((), (), s32[]{:S(2)}) async-start(), calls=%async_computation.3 | async-start | bytes 1228800 | tf_op jit(solution)/shard_map/reduce_scatter | solution.py:37
  73.0 6.8 %copy-start.2 = (s32[16,1]{0,1:T(1,128)S(1)}, s32[16,1]{0,1:T(1,128)}, u32[]{:S(2)}) copy-start(s32[16,1]{0,1:T(1,128)} %param.9) | copy-start | bytes 196
  73.0 7.0 %copy-start.1 = (bf16[256,120]{0,1:T(8,128)(2,1)S(1)}, bf16[256,120]{0,1:T(8,128)(2,1)}, u32[]{:S(2)}) copy-start(bf16[256,120]{0,1:T(8,128)(2,1)} %param.8) | copy-start | bytes 184324
  73.0 17.9 %copy-start = (bf16[4,120,120]{2,1,0:T(8,128)(2,1)S(1)}, bf16[4,120,120]{2,1,0:T(8,128)(2,1)}, u32[]{:S(2)}) copy-start(bf16[4,120,120]{2,1,0:T(8,128)(2,1)} %param.6) | copy-start | bytes 345604
  73.0 63.6 %reduce-scatter.5.cloned.1.call-start = ((), (), s32[]{:S(2)}) async-start(), calls=%async_computation.4 | async-start | bytes 1228800 | tf_op jit(solution)/shard_map/reduce_scatter | solution.py:37
Sparse Core Ops, SparseCore 0:
  9.2 56.9 all-gather.1
  73.2 26.2 reduce-scatter.2
  101.8 34.8 reduce-scatter.4
where the time goes:
time: 177 us
  waiting for transfers between devices  71 us (40%)
  blocking collectives  62.4 us (35%)
  matrix products  19.3 us (11%)
  between operations  13.2 us (7%)
  other arithmetic  8.89 us (5%)
  local copies, waits for them, and re-layouts  2.12 us (1%)
    all_gather x1, waiting for transfers between devices, per_device(): lax.all_gather(cabs_coeff, 'aux', axis=0, tiled=True)  57.3 us
    all_gather x2, blocking collectives, per_device(): spread = lax.all_gather(rounded, 'shell', axis=1, tiled=True)  51.6 us
    dot_general x2, matrix products, per_device(): lax.dot_general(flat, lax.all_gather(cabs_coeff, 'aux', axis=0, tiled=Tru...  13.5 us
    reduce_scatter x2, waiting for transfers between devices, per_device(): lax.psum_scatter(terms.astype(jnp.bfloat16), 'shell', scatter_dimension=1...  12.9 us
    all_gather x1, blocking collectives, per_device(): occ_full = lax.all_gather(occ_coeff, 'aux', axis=0, tiled=True)  10.9 us
    concatenate x1, other arithmetic, per_device(): return jnp.concatenate(results, axis=1)  6.71 us
    dot_general x2, matrix products, per_device(): jnp.einsum('kqiw,mi->kqwm', half_owned, occ_full, preferred_element_type=...  4.81 us
  transfers between devices with their start and end apart: 3, of which 3 were waited for; matrix products, arithmetic and copies ran while one was open for 6% of the time, Pallas kernels for 0%

commit v1 on v0

--- a/solution.py
+++ b/solution.py
@@ -40,7 +40,7 @@
         my_rows = lax.dynamic_slice_in_dim(occ_full, me_shell * share_cols, share_cols, 0)
         occ_term = jnp.einsum("qij,nj->qin", occ_dens, my_rows, preferred_element_type=jnp.float32)
         rounded = (mine + occ_term.reshape(span * NOCC, share_cols)).astype(jnp.bfloat16)
-        spread = lax.all_gather(rounded, "shell", axis=1, tiled=True)
+        spread = jnp.concatenate(lax.all_gather(rounded, "shell"), axis=1)
         blocks = spread.reshape(span, NOCC, ntile, width)
         half_owned = jnp.einsum(
             "kt,qitw->kqiw", select, blocks, preferred_element_type=jnp.float32

time: 177 us -> 178 us (level)
  local copies, waits for them, and re-layouts: 2.12 us -> 3.99 us
where the time goes in v1:
time: 178 us
  waiting for transfers between devices  70.1 us (39%)
  blocking collectives  62.6 us (35%)
  matrix products  19.3 us (11%)
  between operations  13.2 us (7%)
  other arithmetic  8.89 us (5%)
  local copies, waits for them, and re-layouts  3.99 us (2%)
    all_gather x1, waiting for transfers between devices, per_device(): lax.all_gather(cabs_coeff, 'aux', axis=0, tiled=True)  57.3 us
    all_gather x2, blocking collectives, per_device(): spread = jnp.concatenate(lax.all_gather(rounded, 'shell'), axis=1)  51.8 us
    dot_general x2, matrix products, per_device(): lax.dot_general(flat, lax.all_gather(cabs_coeff, 'aux', axis=0, tiled=Tru...  13.5 us
    reduce_scatter x2, waiting for transfers between devices, per_device(): lax.psum_scatter(terms.astype(jnp.bfloat16), 'shell', scatter_dimension=1...  12 us
    all_gather x1, blocking collectives, per_device(): occ_full = lax.all_gather(occ_coeff, 'aux', axis=0, tiled=True)  10.9 us
    concatenate x1, other arithmetic, per_device(): return jnp.concatenate(results, axis=1)  6.71 us
    dot_general x2, matrix products, per_device(): jnp.einsum('kqiw,mi->kqwm', half_owned, occ_full, preferred_element_type=...  4.81 us
  transfers between devices with their start and end apart: 3, of which 3 were waited for; matrix products, arithmetic and copies ran while one was open for 6% of the time, Pallas kernels for 0%

profile of v1, /device:TPU:0, one launch (start us, length us, event | category | flops | bytes accessed | tf_op | source)
XLA Modules:
  0.0 178.1 jit_solution(10119550829804551322)
XLA Ops:
  6.5 0.0 all-gather.4.cloned.1.call-start
  6.5 0.7 all-gather.4.cloned.1.call-update
  7.3 0.0 reduce-scatter.3.cloned.1.call-start
  7.3 1.6 fusion.24
  8.9 57.3 %all-gather.4.cloned.1.call-done = bf16[2048,2048]{1,0:T(8,128)(2,1)} async-done(((bf16[256,2048]{1,0:T(8,128)(2,1)}), bf16[2048,2048]{1,0:T(8,128)(2,1)}) %all-gather.4.cloned.1.call-update) | async-done | bytes 8388624 | tf_op jit(solution)/shard_map/all_gather | solution.py:33
  66.2 6.8 %convolution_convert_fusion.3 = bf16[240,2048]{1,0:T(8,128)(2,1)} fusion(bf16[240,2048]{1,0:T(8,128)(2,1)S(1)} %bitcast.53, bf16[2048,2048]{1,0:T(8,128)(2,1)} %all-gather.4.cloned.1.call-done), kind=kOutput, calls=%fused_computation.4 | convolution fusion | flops 2013757440 | bytes 10354688 | tf_op jit(solution)/shard_map/dot_general | solution.py:31
  73.0 0.0 reduce-scatter.3.cloned.1.call-update
  73.0 0.0 reduce-scatter.5.cloned.1.call-start
  73.1 6.7 %convolution_convert_fusion.2 = bf16[240,2048]{1,0:T(8,128)(2,1)} fusion(bf16[240,2048]{1,0:T(8,128)(2,1)S(1)} %bitcast.52, bf16[2048,2048]{1,0:T(8,128)(2,1)} %all-gather.4.cloned.1.call-done), kind=kOutput, calls=%fused_computation.3 | convolution fusion | flops 2013757440 | bytes 10354688 | tf_op jit(solution)/shard_map/dot_general | solution.py:31
  79.8 0.0 reduce-scatter.5.cloned.1.call-update
  79.8 0.0 copy-done.2
  79.9 0.1 copy.7
  80.0 0.0 copy-done.1
  80.0 10.9 %all_gather.20 = bf16[2048,120]{0,1:T(8,128)(2,1)S(1)} all-gather(bf16[256,120]{0,1:T(8,128)(2,1)S(1)} %copy-done.1), channel_id=1, replica_groups=mesh['aux'=8,'shell'=4] {'aux'}, dimensions={0}, use_global_device_ids=true | all-gather | bytes 552960 | tf_op jit(solution)/shard_map/all_gather | solution.py:14
  90.8 0.1 add_reduce_fusion
  91.0 0.2 fusion.4
  91.2 0.2 fusion.6
  91.4 8.0 %reduce-scatter.3.cloned.1.call-done = bf16[240,512]{1,0:T(8,128)(2,1)} async-done(((bf16[240,2048]{1,0:T(8,128)(2,1)}), bf16[240,512]{1,0:T(8,128)(2,1)}) %reduce-scatter.3.cloned.1.call-update) | async-done | bytes 245776 | tf_op jit(solution)/shard_map/reduce_scatter | solution.py:37
  99.4 1.0 fusion.1
  100.5 31.1 %all-gather = bf16[960,512]{1,0:T(8,128)(2,1)S(1)} all-gather(bf16[240,512]{1,0:T(8,128)(2,1)S(1)} %fusion.1), channel_id=2, replica_groups=mesh['aux'=8,'shell'=4] {'shell'}, dimensions={0}, use_global_device_ids=true | all-gather | bytes 1228800 | tf_op jit(solution)/shard_map/all_gather | solution.py:43
  131.6 0.8 copy.21
  132.3 0.4 reshape_reshape.6
  132.7 4.0 %reduce-scatter.5.cloned.1.call-done = bf16[240,512]{1,0:T(8,128)(2,1)} async-done(((bf16[240,2048]{1,0:T(8,128)(2,1)}), bf16[240,512]{1,0:T(8,128)(2,1)}) %reduce-scatter.5.cloned.1.call-update) | async-done | bytes 245776 | tf_op jit(solution)/shard_map/reduce_scatter | solution.py:37
  136.7 1.0 fusion
  137.7 20.7 %all-gather.1 = bf16[960,512]{1,0:T(8,128)(2,1)S(1)} all-gather(bf16[240,512]{1,0:T(8,128)(2,1)S(1)} %fusion), channel_id=3, replica_groups=mesh['aux'=8,'shell'=4] {'shell'}, dimensions={0}, use_global_device_ids=true | all-gather | bytes 1228800 | tf_op jit(solution)/shard_map/all_gather | solution.py:43
  158.4 0.8 copy.20
  159.1 0.4 reshape_reshape.7
  159.5 0.3 fusion.16
  159.8 0.3 fusion.14
  160.1 2.4 %convolution_convert_fusion = bf16[8,2,128,2048]{3,2,1,0:T(8,128)(2,1)S(1)} fusion(bf16[8,2,120,128]{3,0,2,1:T(8,128)(2,1)S(1)} %fusion.14, bf16[2048,120]{0,1:T(8,128)(2,1)S(1)} %all_gather.20), kind=kOutput, calls=%fused_computation.1 | convolution fusion | flops 1010827264 | bytes 9371648 | tf_op jit(solution)/shard_map/kqiw,mi->kqwm/dot_general | solution.py:48
  162.5 2.4 %convolution_convert_fusion.1 = bf16[8,2,128,2048]{3,2,1,0:T(8,128)(2,1)S(1)} fusion(bf16[8,2,120,128]{3,0,2,1:T(8,128)(2,1)S(1)} %fusion.16, bf16[2048,120]{0,1:T(8,128)(2,1)S(1)} %all_gather.20), kind=kOutput, calls=%fused_computation.2 | convolution fusion | flops 1010827264 | bytes 9371648 | tf_op jit(solution)/shard_map/kqiw,mi->kqwm/dot_general | solution.py:48
  164.9 6.7 %pad_maximum_fusion = bf16[8,4,128,2048]{3,2,1,0:T(8,128)(2,1)} fusion(bf16[8,2,128,2048]{3,2,1,0:T(8,128)(2,1)S(1)} %convolution_convert_fusion, bf16[8,2,128,2048]{3,2,1,0:T(8,128)(2,1)S(1)} %convolution_convert_fusion.1), kind=kLoop, calls=%fused_computation | loop fusion | flops 8388608 | bytes 33554432 | tf_op jit(solution)/shard_map/concatenate | solution.py:52
  (6 shorter events, 0.0 us)
Async XLA Ops:
  6.5 59.7 %all-gather.4.cloned.1.call-start = ((), (), s32[]{:S(2)}) async-start(), calls=%async_computation.2 | async-start | bytes 9437184 | tf_op jit(solution)/shard_map/all_gather | solution.py:33
  7.3 92.2 %reduce-scatter.3.cloned.1.call-start = ((), (), s32[]{:S(2)}) async-start(), calls=%async_computation.3 | async-start | bytes 1228800 | tf_op jit(solution)/shard_map/reduce_scatter | solution.py:37
  73.0 6.8 %copy-start.2 = (s32[16,1]{0,1:T(1,128)S(1)}, s32[16,1]{0,1:T(1,128)}, u32[]{:S(2)}) copy-start(s32[16,1]{0,1:T(1,128)} %param.9) | copy-start | bytes 196
  73.0 7.0 %copy-start.1 = (bf16[256,120]{0,1:T(8,128)(2,1)S(1)}, bf16[256,120]{0,1:T(8,128)(2,1)}, u32[]{:S(2)}) copy-start(bf16[256,120]{0,1:T(8,128)(2,1)} %param.8) | copy-start | bytes 184324
  73.0 17.9 %copy-start = (bf16[4,120,120]{2,1,0:T(8,128)(2,1)S(1)}, bf16[4,120,120]{2,1,0:T(8,128)(2,1)}, u32[]{:S(2)}) copy-start(bf16[4,120,120]{2,1,0:T(8,128)(2,1)} %param.6) | copy-start | bytes 345604
  73.0 63.6 %reduce-scatter.5.cloned.1.call-start = ((), (), s32[]{:S(2)}) async-start(), calls=%async_computation.4 | async-start | bytes 1228800 | tf_op jit(solution)/shard_map/reduce_scatter | solution.py:37
Sparse Core Ops, SparseCore 0:
  9.2 56.9 all-gather.3
  73.2 26.2 reduce-scatter.2
  101.8 34.8 reduce-scatter.4
